TPU v7x, 32 devices: a whole 2x2x4 slice. The times are simulated.
32 devices in a mesh: dp: 8 (over y, x, core), mp: 4 (over z).
Axes of the slice: x: 2, y: 2, z: 4, core: 2. Of those that a mesh axis runs over, the one named last changes fastest.
Arguments:
- tokens: bfloat16 [32768, 1024], P('dp', 'mp'), may hold values from -6 to 6
- cotangent: bfloat16 [32768, 1024], P('dp', 'mp'), may hold values from -6 to 6
- norm_gain: float32 [1024], P('mp'), may hold values from 0.5 to 1.5
- ema_delta: float32 [1024, 16], P('mp'), may hold values from -4 to 2
- ema_alpha: float32 [1024, 16], P('mp'), may hold values from -1.5 to 2
- ema_beta: float32 [1024, 16], P('mp'), may hold values from -4 to 4
- ema_eta: float32 [1024, 16], P('mp'), may hold values from -1.5 to 1.5
- ema_omega: float32 [1024], P('mp'), may hold values from -4 to 4
- shared_proj: bfloat16 [1024, 128], replicated, may hold values from -0.1875 to 0.1875
- query_gain: float32 [128], replicated, may hold values from -8 to 8
- query_bias: float32 [128], replicated, may hold values from -4 to 4
- key_gain: float32 [128], replicated, may hold values from -8 to 8
- value_proj: bfloat16 [1024, 2048], P(None, 'mp'), may hold values from -0.1875 to 0.1875
- gate_proj: bfloat16 [1024, 2048], P(None, 'mp'), may hold values from -0.1875 to 0.1875
- mixer_proj: bfloat16 [1024, 1024], P(None, 'mp'), may hold values from -0.1875 to 0.1875
- update_proj: bfloat16 [1024, 1024], P(None, 'mp'), may hold values from -0.1875 to 0.1875
- output_proj: bfloat16 [2048, 1024], P('mp'), may hold values from -0.5 to 0.5
- ffn_gain: float32 [1024], P('mp'), may hold values from 0.5 to 1.5
- up_proj: bfloat16 [1024, 4096], P(None, 'mp'), may hold values from -0.1875 to 0.1875
- down_proj: bfloat16 [4096, 1024], P('mp'), may hold values from -0.09375 to 0.09375
Outputs:
- layer_out: bfloat16 [32768, 1024], P('dp', 'mp')
- token_grad: bfloat16 [32768, 1024], P('dp', 'mp')
- gain_grad: float32 [1024], P('mp')
- delta_grad: float32 [1024, 16], P('mp')
- alpha_grad: float32 [1024, 16], P('mp')
- beta_grad: float32 [1024, 16], P('mp')
- eta_grad: float32 [1024, 16], P('mp')
- omega_grad: float32 [1024], P('mp')
- shared_grad: float32 [1024, 128], replicated
- query_grad: float32 [128], replicated
- bias_grad: float32 [128], replicated
- key_grad: float32 [128], replicated
- value_grad: float32 [1024, 2048], P(None, 'mp')
- gate_grad: float32 [1024, 2048], P(None, 'mp')
- mixer_grad: float32 [1024, 1024], P(None, 'mp')
- update_grad: float32 [1024, 1024], P(None, 'mp')
- output_grad: float32 [2048, 1024], P('mp')
- ffn_grad: float32 [1024], P('mp')
- up_grad: float32 [1024, 4096], P(None, 'mp')
- down_grad: float32 [4096, 1024], P('mp')
All inputs are finite; a program needn't handle non-finite values.
Results may differ from a plain program's by a relative error of at most 0.0307.
Values may be sent and summed in bfloat16 or wider, within the bound.
A program may use at most 384 MiB of HBM per device.

v0:
```python
import jax
import jax.numpy as jnp
from jax import lax
from jax.sharding import PartitionSpec as P

D = 1024
GROUP = 128
LEN = 2048
MICRO = 2
EPS = 1e-05


def matmul(left, right):
    return jnp.dot(left, right, preferred_element_type=jnp.float32)


def matmul_tn(left, right):
    return lax.dot_general(
        left, right, (((0,), (0,)), ((), ())), preferred_element_type=jnp.float32
    )


def matmul_nt(left, right):
    return lax.dot_general(
        left, right, (((1,), (1,)), ((), ())), preferred_element_type=jnp.float32
    )


def silu_slope(values):
    logistic = jax.nn.sigmoid(values)
    return logistic * (1.0 + values * (1.0 - logistic))


def norm_forward(shard, gain):
    total, power = lax.psum((jnp.sum(shard, axis=1), jnp.sum(shard * shard, axis=1)), "mp")
    mean_row = total / D
    scale = lax.rsqrt(power / D - mean_row * mean_row + EPS)
    normed = (shard - mean_row[:, None]) * scale[:, None]
    return (normed, scale, (normed * gain).astype(jnp.bfloat16))


def norm_backward(grad, normed, scale, gain):
    gain_part = jnp.sum(grad * normed, axis=0)
    scaled = grad * gain
    first, second = lax.psum((jnp.sum(scaled, axis=1), jnp.sum(scaled * normed, axis=1)), "mp")
    back = scale[:, None] * (scaled - (first / D)[:, None] - normed * (second / D)[:, None])
    return (back, gain_part)


def ema_local(signal, delta, alpha, beta, eta):
    rate = jax.nn.sigmoid(delta)
    keep_log = jnp.log(1.0 - rate * jax.nn.sigmoid(alpha))
    push = rate * beta
    width = signal.shape[1]
    blocks = signal.reshape(-1, LEN // GROUP, GROUP, width)
    offsets = jnp.arange(GROUP, dtype=jnp.float32)
    powers = jnp.exp(offsets[:, None, None] * keep_log[None])
    kernel = jnp.sum(powers * (push * eta)[None], axis=2)
    lag = jnp.arange(GROUP)[:, None] - jnp.arange(GROUP)[None, :]
    toeplitz = jnp.where((lag >= 0)[:, :, None], jnp.take(kernel, jnp.maximum(lag, 0), axis=0), 0.0)
    inner = jnp.einsum("tsc,gbsc->gbtc", toeplitz, blocks, precision=lax.Precision.HIGHEST)
    tail = jnp.exp((GROUP - 1.0 - offsets)[:, None, None] * keep_log[None]) * push[None]
    ends = jnp.einsum("gbsc,scj->bgcj", blocks, tail, precision=lax.Precision.HIGHEST)
    carry_keep = jnp.exp(GROUP * keep_log)

    def advance(state, end_now):
        return (carry_keep * state + end_now, state)

    _, starts = lax.scan(advance, jnp.zeros(ends.shape[1:], jnp.float32), ends)
    lead = jnp.exp((offsets + 1.0)[:, None, None] * keep_log[None]) * eta[None]
    outer = jnp.einsum("tcj,bgcj->gbtc", lead, starts, precision=lax.Precision.HIGHEST)
    return (inner + outer).reshape(signal.shape)


def group_scores(query, keys):
    blocks = query.shape[0] // GROUP
    query_blocks = query.reshape(blocks, GROUP, query.shape[1])
    key_blocks = keys.reshape(blocks, GROUP, keys.shape[1])
    raw = jnp.einsum("nqz,nkz->nqk", query_blocks, key_blocks, preferred_element_type=jnp.float32)
    raw = raw * query.shape[1] ** (-0.5)
    place = jnp.arange(GROUP)
    return jnp.where((place[:, None] >= place[None, :])[None], raw, -1e30)


def local(
    tokens,
    cotangent,
    norm_gain,
    ema_delta,
    ema_alpha,
    ema_beta,
    ema_eta,
    ema_omega,
    shared_proj,
    query_gain,
    query_bias,
    key_gain,
    value_proj,
    gate_proj,
    mixer_proj,
    update_proj,
    output_proj,
    ffn_gain,
    up_proj,
    down_proj,
):
    width = tokens.shape[1]
    rows_micro = tokens.shape[0] // MICRO
    shared_rows = lax.dynamic_slice_in_dim(shared_proj, lax.axis_index("mp") * width, width, 0)
    head_scale = query_gain.shape[0] ** (-0.5)
    mixer_totals_list = tuple(
        (
            jnp.zeros(item.shape, jnp.float32)
            for item in (
                norm_gain,
                ema_delta,
                ema_alpha,
                ema_beta,
                ema_eta,
                ema_omega,
                shared_proj,
                query_gain,
                query_bias,
                key_gain,
                value_proj,
                gate_proj,
                mixer_proj,
                update_proj,
                output_proj,
            )
        )
    )
    ffn_sums = tuple(
        (jnp.zeros(item.shape, jnp.float32) for item in (ffn_gain, up_proj, down_proj))
    )
    layer_rows = []
    token_rows = []
    for batch_index in range(MICRO):
        first_row = batch_index * rows_micro
        inputs = lax.slice_in_dim(tokens, first_row, first_row + rows_micro, axis=0).astype(
            jnp.float32
        )
        grad_out = lax.slice_in_dim(cotangent, first_row, first_row + rows_micro, axis=0)
        normed_one, scale_one, normed_low = norm_forward(inputs, norm_gain)
        signal = normed_low.astype(jnp.float32)
        ema_value, ema_pull = jax.vjp(ema_local, signal, ema_delta, ema_alpha, ema_beta, ema_eta)
        mix_pre = ema_value + ema_omega * signal
        mixed_low = jax.nn.silu(mix_pre).astype(jnp.bfloat16)
        normed_all, mixed_all = (
            lax.all_gather(normed_low, "mp", axis=1, tiled=True),
            lax.all_gather(mixed_low, "mp", axis=1, tiled=True),
        )
        shared_pre = matmul(mixed_all, shared_proj)
        shared = jax.nn.silu(shared_pre)
        query = (shared * query_gain + query_bias).astype(jnp.bfloat16)
        keys = (shared * key_gain).astype(jnp.bfloat16)
        value_pre = matmul(normed_all, value_proj)
        values = jax.nn.silu(value_pre).astype(jnp.bfloat16)
        gate_pre = matmul(mixed_all, gate_proj)
        gate = jax.nn.silu(gate_pre)
        scores = group_scores(query, keys)
        peak = jnp.max(scores, axis=-1, keepdims=True)
        weights = jnp.exp(scores - peak)
        weight_sum = jnp.sum(weights, axis=-1, keepdims=True)
        log_total = peak + jnp.log(weight_sum)
        probabilities = weights / weight_sum
        blocks = probabilities.shape[0]
        value_block_rows = values.reshape(blocks, GROUP, values.shape[1])
        attention_result = jnp.einsum(
            "dzc,dcs->dzs",
            probabilities.astype(jnp.bfloat16),
            value_block_rows,
            preferred_element_type=jnp.float32,
        ).reshape(rows_micro, values.shape[1])
        hidden = (gate * attention_result).astype(jnp.bfloat16)
        attn_out = lax.psum_scatter(
            matmul(hidden, output_proj).astype(jnp.bfloat16), "mp", scatter_dimension=1, tiled=True
        ).astype(jnp.float32)
        update = jax.nn.sigmoid(matmul(mixed_all, update_proj))
        act_pre = matmul(mixed_all, mixer_proj) + attn_out
        act_value = jax.nn.silu(act_pre)
        middle = update * act_value + (1.0 - update) * inputs
        normed_two, scale_two, ffn_low = norm_forward(middle, ffn_gain)
        ffn_all = lax.all_gather(ffn_low, "mp", axis=1, tiled=True)
        up_pre = matmul(ffn_all, up_proj)
        upper = jax.nn.silu(up_pre).astype(jnp.bfloat16)
        down_out = lax.psum_scatter(
            matmul(upper, down_proj).astype(jnp.bfloat16), "mp", scatter_dimension=1, tiled=True
        ).astype(jnp.float32)
        layer_rows.append((middle + down_out).astype(jnp.bfloat16))
        grad_all = lax.all_gather(grad_out, "mp", axis=1, tiled=True)
        down_part = matmul_tn(upper, grad_all)
        d_up_pre = (matmul_nt(grad_all, down_proj) * silu_slope(up_pre)).astype(jnp.bfloat16)
        up_part = matmul_tn(ffn_all, d_up_pre)
        d_ffn_in = lax.psum_scatter(
            matmul_nt(d_up_pre, up_proj).astype(jnp.bfloat16), "mp", scatter_dimension=1, tiled=True
        ).astype(jnp.float32)
        d_middle, ffn_gain_part = norm_backward(d_ffn_in, normed_two, scale_two, ffn_gain)
        d_middle = d_middle + grad_out.astype(jnp.float32)
        ffn_sums = (ffn_sums[0] + ffn_gain_part, ffn_sums[1] + up_part, ffn_sums[2] + down_part)
        if batch_index == MICRO - 1:
            ffn_reduced = ffn_sums
        d_update_pre = (d_middle * (act_value - inputs) * update * (1.0 - update)).astype(
            jnp.bfloat16
        )
        d_act_pre = (d_middle * update * silu_slope(act_pre)).astype(jnp.bfloat16)
        d_inputs = d_middle * (1.0 - update)
        mixer_part = matmul_tn(mixed_all, d_act_pre)
        update_part = matmul_tn(mixed_all, d_update_pre)
        d_act_all = lax.all_gather(d_act_pre, "mp", axis=1, tiled=True)
        output_part = matmul_tn(hidden, d_act_all)
        d_hidden = matmul_nt(d_act_all, output_proj)
        d_gate_pre = (d_hidden * attention_result * silu_slope(gate_pre)).astype(jnp.bfloat16)
        d_attended = (d_hidden * gate).astype(jnp.bfloat16)
        attention_result_blocks = d_attended.reshape(blocks, GROUP, d_attended.shape[1])
        probs_again = jnp.exp(group_scores(query, keys) - log_total)
        d_probs = lax.psum(
            jnp.einsum(
                "gas,gcs->gac",
                attention_result_blocks,
                value_block_rows,
                preferred_element_type=jnp.float32,
            ).astype(jnp.bfloat16),
            "mp",
        ).astype(jnp.float32)
        d_value = jnp.einsum(
            "uhi,uhs->uis",
            probs_again.astype(jnp.bfloat16),
            attention_result_blocks,
            preferred_element_type=jnp.float32,
        ).reshape(rows_micro, values.shape[1])
        d_value_pre = (d_value * silu_slope(value_pre)).astype(jnp.bfloat16)
        d_scores = probs_again * (d_probs - jnp.sum(probs_again * d_probs, axis=-1, keepdims=True))
        d_scores_low = d_scores.astype(jnp.bfloat16)
        query_blocks = query.reshape(blocks, GROUP, query.shape[1])
        key_blocks = keys.reshape(blocks, GROUP, keys.shape[1])
        d_query = (
            jnp.einsum(
                "nqk,nkz->nqz", d_scores_low, key_blocks, preferred_element_type=jnp.float32
            ).reshape(rows_micro, -1)
            * head_scale
        )
        d_keys = (
            jnp.einsum(
                "nqk,nqz->nkz", d_scores_low, query_blocks, preferred_element_type=jnp.float32
            ).reshape(rows_micro, -1)
            * head_scale
        )
        query_part = jnp.sum(d_query * shared, axis=0)
        bias_part = jnp.sum(d_query, axis=0)
        key_part = jnp.sum(d_keys * shared, axis=0)
        d_shared_pre = ((d_query * query_gain + d_keys * key_gain) * silu_slope(shared_pre)).astype(
            jnp.bfloat16
        )
        shared_part = matmul_tn(mixed_all, d_shared_pre)
        value_part = matmul_tn(normed_all, d_value_pre)
        gate_part = matmul_tn(mixed_all, d_gate_pre)
        mixed_terms = matmul_nt(d_gate_pre, gate_proj) + matmul_nt(d_update_pre, update_proj)
        mixed_terms = mixed_terms + matmul_nt(d_act_pre, mixer_proj)
        normed_terms = matmul_nt(d_value_pre, value_proj)
        d_mixed, d_normed = (
            lax.psum_scatter(
                mixed_terms.astype(jnp.bfloat16), "mp", scatter_dimension=1, tiled=True
            ).astype(jnp.float32),
            lax.psum_scatter(
                normed_terms.astype(jnp.bfloat16), "mp", scatter_dimension=1, tiled=True
            ).astype(jnp.float32),
        )
        d_mixed = d_mixed + matmul_nt(d_shared_pre, shared_rows)
        d_mix_pre = d_mixed * silu_slope(mix_pre)
        omega_part = jnp.sum(d_mix_pre * signal, axis=0)
        d_signal, delta_part, alpha_part, beta_part, eta_part = ema_pull(d_mix_pre)
        d_normed = d_normed + d_signal + d_mix_pre * ema_omega
        d_tokens, gain_part = norm_backward(d_normed, normed_one, scale_one, norm_gain)
        token_rows.append((d_inputs + d_tokens).astype(jnp.bfloat16))
        summand_terms = (
            gain_part,
            delta_part,
            alpha_part,
            beta_part,
            eta_part,
            omega_part,
            shared_part,
            query_part,
            bias_part,
            key_part,
            value_part,
            gate_part,
            mixer_part,
            update_part,
            output_part,
        )
        mixer_totals_list = tuple(
            (
                running_total + summand_term
                for running_total, summand_term in zip(mixer_totals_list, summand_terms)
            )
        )
    reduced = lax.psum(
        (
            mixer_totals_list[0],
            mixer_totals_list[1],
            mixer_totals_list[2],
            mixer_totals_list[3],
            mixer_totals_list[4],
            mixer_totals_list[5],
            mixer_totals_list[6],
            mixer_totals_list[7],
            mixer_totals_list[8],
            mixer_totals_list[9],
            mixer_totals_list[10],
            mixer_totals_list[11],
            mixer_totals_list[12],
            mixer_totals_list[13],
            mixer_totals_list[14],
            ffn_sums[0],
            ffn_sums[1],
            ffn_sums[2],
        ),
        "dp",
    )
    mixer_reduced = reduced[:15]
    ffn_reduced = reduced[15:]
    layer_out = jnp.concatenate(layer_rows, axis=0)
    token_grad = jnp.concatenate(token_rows, axis=0)
    return (
        layer_out,
        token_grad,
        mixer_reduced[0],
        mixer_reduced[1],
        mixer_reduced[2],
        mixer_reduced[3],
        mixer_reduced[4],
        mixer_reduced[5],
        mixer_reduced[6],
        mixer_reduced[7],
        mixer_reduced[8],
        mixer_reduced[9],
        mixer_reduced[10],
        mixer_reduced[11],
        mixer_reduced[12],
        mixer_reduced[13],
        mixer_reduced[14],
        ffn_reduced[0],
        ffn_reduced[1],
        ffn_reduced[2],
    )


def solution(mesh):
    in_specs = (
        P("dp", "mp"),
        P("dp", "mp"),
        P("mp"),
        P("mp", None),
        P("mp", None),
        P("mp", None),
        P("mp", None),
        P("mp"),
        P(),
        P(),
        P(),
        P(),
        P(None, "mp"),
        P(None, "mp"),
        P(None, "mp"),
        P(None, "mp"),
        P("mp", None),
        P("mp"),
        P(None, "mp"),
        P("mp", None),
    )
    out_specs = (
        P("dp", "mp"),
        P("dp", "mp"),
        P("mp"),
        P("mp", None),
        P("mp", None),
        P("mp", None),
        P("mp", None),
        P("mp"),
        P(),
        P(),
        P(),
        P(),
        P(None, "mp"),
        P(None, "mp"),
        P(None, "mp"),
        P(None, "mp"),
        P("mp", None),
        P("mp"),
        P(None, "mp"),
        P("mp", None),
    )
    return jax.shard_map(local, mesh=mesh, in_specs=in_specs, out_specs=out_specs, check_vma=False)
```

profile of v0, /device:TPU:0, one launch (start us, length us, event | category | flops | bytes accessed | tf_op | source)
XLA Modules:
  0.0 2425.9 jit_solution(17531408031681746158)
XLA Ops:
  15.4 21.4 all-reduce.5
  55.5 66.9 %gather_fusion = f32[16384,256]{1,0:T(8,128)} fusion(f32[128,256]{1,0:T(8,128)S(1)} %copy.189, s32[16384]{0:T(1024)} %broadcast_clamp_fusion), kind=kCustom, calls=%fused_computation.clone | custom fusion | bytes 33619968 | tf_op jit(solution)/shard_map/jvp(jit(_take))/gather | solution.py:60
  122.4 18.1 copy.190
  140.6 20.4 fusion.2
  179.8 21.2 while.64
  208.5 21.2 while.65
  262.0 76.3 %all-gather.11.cloned.1.call-done = bf16[2048,1024]{1,0:T(8,128)(2,1)} async-done(((bf16[2048,256]{1,0:T(8,128)(2,1)}), bf16[2048,1024]{1,0:T(8,128)(2,1)}) %all-gather.11.cloned.1.call-update) | async-done | bytes 4194320 | tf_op jit(solution)/shard_map/all_gather | solution.py:151
  341.8 77.5 %all-gather.17.cloned.1.call-done = bf16[2048,1024]{1,0:T(8,128)(2,1)} async-done(((bf16[2048,256]{1,0:T(8,128)(2,1)}), bf16[2048,1024]{1,0:T(8,128)(2,1)}) %all-gather.17.cloned.1.call-update) | async-done | bytes 4194320 | tf_op jit(solution)/shard_map/all_gather | solution.py:151
  425.6 74.6 %all-gather.19.cloned.1.call-done = bf16[2048,1024]{1,0:T(8,128)(2,1)} async-done(((bf16[2048,256]{1,0:T(8,128)(2,1)}), bf16[2048,1024]{1,0:T(8,128)(2,1)}) %all-gather.19.cloned.1.call-update) | async-done | bytes 4194320 | tf_op jit(solution)/shard_map/all_gather | solution.py:150
  524.1 56.2 %all-gather.13.cloned.1.call-done = bf16[2048,1024]{1,0:T(8,128)(2,1)} async-done(((bf16[2048,256]{1,0:T(8,128)(2,1)}), bf16[2048,1024]{1,0:T(8,128)(2,1)}) %all-gather.13.cloned.1.call-update) | async-done | bytes 4194320 | tf_op jit(solution)/shard_map/all_gather | solution.py:150
  608.0 49.4 %reduce-scatter.15.cloned.1.call-done = bf16[2048,256]{1,0:T(8,128)(2,1)} async-done(((bf16[2048,1024]{1,0:T(8,128)(2,1)}), bf16[2048,256]{1,0:T(8,128)(2,1)}) %reduce-scatter.15.cloned.1.call-update) | async-done | bytes 1048592 | tf_op jit(solution)/shard_map/reduce_scatter | solution.py:176
  662.5 74.5 %reduce-scatter.11.cloned.1.call-done = bf16[2048,256]{1,0:T(8,128)(2,1)} async-done(((bf16[2048,1024]{1,0:T(8,128)(2,1)}), bf16[2048,256]{1,0:T(8,128)(2,1)}) %reduce-scatter.11.cloned.1.call-update) | async-done | bytes 1048592 | tf_op jit(solution)/shard_map/reduce_scatter | solution.py:176
  748.6 18.2 all-reduce.4
  773.2 75.6 %all-gather.15.cloned.1.call-done = bf16[2048,1024]{1,0:T(8,128)(2,1)} async-done(((bf16[2048,256]{1,0:T(8,128)(2,1)}), bf16[2048,1024]{1,0:T(8,128)(2,1)}) %all-gather.15.cloned.1.call-update) | async-done | bytes 4194320 | tf_op jit(solution)/shard_map/all_gather | solution.py:184
  859.5 69.6 %all-gather.23.cloned.1.call-done = bf16[2048,1024]{1,0:T(8,128)(2,1)} async-done(((bf16[2048,256]{1,0:T(8,128)(2,1)}), bf16[2048,1024]{1,0:T(8,128)(2,1)}) %all-gather.23.cloned.1.call-update) | async-done | bytes 4194320 | tf_op jit(solution)/shard_map/all_gather | solution.py:191
  949.5 74.8 %reduce-scatter.19.cloned.1.call-done = bf16[2048,256]{1,0:T(8,128)(2,1)} async-done(((bf16[2048,1024]{1,0:T(8,128)(2,1)}), bf16[2048,256]{1,0:T(8,128)(2,1)}) %reduce-scatter.19.cloned.1.call-update) | async-done | bytes 1048592 | tf_op jit(solution)/shard_map/reduce_scatter | solution.py:195
  1030.0 80.4 %all-gather.21.cloned.1.call-done = bf16[2048,1024]{1,0:T(8,128)(2,1)} async-done(((bf16[2048,256]{1,0:T(8,128)(2,1)}), bf16[2048,1024]{1,0:T(8,128)(2,1)}) %all-gather.21.cloned.1.call-update) | async-done | bytes 4194320 | tf_op jit(solution)/shard_map/all_gather | solution.py:184
  1119.4 71.4 %all-gather.27.cloned.1.call-done = bf16[2048,1024]{1,0:T(8,128)(2,1)} async-done(((bf16[2048,256]{1,0:T(8,128)(2,1)}), bf16[2048,1024]{1,0:T(8,128)(2,1)}) %all-gather.27.cloned.1.call-update) | async-done | bytes 4194320 | tf_op jit(solution)/shard_map/all_gather | solution.py:191
  1211.4 74.8 %reduce-scatter.25.cloned.1.call-done = bf16[2048,256]{1,0:T(8,128)(2,1)} async-done(((bf16[2048,1024]{1,0:T(8,128)(2,1)}), bf16[2048,256]{1,0:T(8,128)(2,1)}) %reduce-scatter.25.cloned.1.call-update) | async-done | bytes 1048592 | tf_op jit(solution)/shard_map/reduce_scatter | solution.py:195
  1289.5 18.2 all-reduce.3
  1326.6 66.7 %all-gather.29.cloned.1.call-done = bf16[2048,1024]{1,0:T(8,128)(2,1)} async-done(((bf16[2048,256]{1,0:T(8,128)(2,1)}), bf16[2048,1024]{1,0:T(8,128)(2,1)}) %all-gather.29.cloned.1.call-update) | async-done | bytes 4194320 | tf_op jit(solution)/shard_map/all_gather | solution.py:210
  1404.4 69.1 %all-gather.25.cloned.1.call-done = bf16[2048,1024]{1,0:T(8,128)(2,1)} async-done(((bf16[2048,256]{1,0:T(8,128)(2,1)}), bf16[2048,1024]{1,0:T(8,128)(2,1)}) %all-gather.25.cloned.1.call-update) | async-done | bytes 4194320 | tf_op jit(solution)/shard_map/all_gather | solution.py:210
  1645.6 23.4 while.67
  1669.0 24.7 %reduce-scatter.23.cloned.1.call-done = bf16[2048,256]{1,0:T(8,128)(2,1)} async-done(((bf16[2048,1024]{1,0:T(8,128)(2,1)}), bf16[2048,256]{1,0:T(8,128)(2,1)}) %reduce-scatter.23.cloned.1.call-update) | async-done | bytes 1048592 | tf_op jit(solution)/shard_map/reduce_scatter | solution.py:262
  1708.6 23.4 while.66
  1734.5 17.7 fusion
  1806.1 17.9 copy.254
  1823.9 99.6 %scatter_custom_fusion = f32[128,256]{1,0:T(8,128)} fusion(s32[16384]{0:T(1024)S(1)} %fusion.236, f32[16384,256]{1,0:T(8,128)} %bitcast.424, f32[]{:T(128)} %constant.164.clone.1), kind=kCustom, calls=%fused_computation.354 | custom fusion | flops 4194304 | bytes 131584 | tf_op jit(solution)/shard_map/transpose(jvp(jit(_take)))/scatter-add | solution.py:60
  1942.1 17.9 copy.255
  1960.0 99.4 %scatter_custom_fusion.1 = f32[128,256]{1,0:T(8,128)} fusion(s32[16384]{0:T(1024)S(1)} %fusion.236, f32[16384,256]{1,0:T(8,128)} %bitcast.423, f32[]{:T(128)} %constant.164.clone.1), kind=kCustom, calls=%fused_computation.352 | custom fusion | flops 4194304 | bytes 131584 | tf_op jit(solution)/shard_map/transpose(jvp(jit(_take)))/scatter-add | solution.py:60
  2107.4 18.5 all-reduce.2
  2155.8 233.3 %all-reduce.13.cloned.1.call-done = (f32[1024,128]{1,0:T(8,128)}, f32[1024,512]{1,0:T(8,128)}, f32[1024,512]{1,0:T(8,128)}, f32[1024,256]{1,0:T(8,128)}, f32[102...) async-done(((f32[1024,128]{1,0:T(8,128)}, f32[1024,512]{1,0:T(8,128)}, f32[1024,512]{1,0:T(8,128)}, f32[1024,256]{1,0:T(8,128)}, ...) | async-done | bytes 17301520 | tf_op jit(solution)/shard_map/psum | solution.py:299
  (789 shorter events, 726.3 us)
Async XLA Ops:
  7.2 841.6 %copy-start = (bf16[1024,1024]{1,0:T(8,128)(2,1)S(1)}, bf16[1024,1024]{1,0:T(8,128)(2,1)}, u32[]{:S(2)}) copy-start(bf16[1024,1024]{1,0:T(8,128)(2,1)} %param.48) | copy-start | bytes 6291460
  7.3 331.0 %all-gather.11.cloned.1.call-start = ((), (), s32[]{:S(2)}) async-start(), calls=%async_computation.10 | async-start | bytes 5242880 | tf_op jit(solution)/shard_map/all_gather | solution.py:151
  12.0 231.4 %copy-start.69 = (f32[256,16]{1,0:T(8,128)}, f32[256,16]{1,0:T(8,128)S(1)}, u32[]{:S(2)}) copy-start(f32[256,16]{1,0:T(8,128)S(1)} %copy.195) | copy-start | bytes 49156
  12.7 230.6 %copy-start.47 = (f32[256,16]{1,0:T(8,128)}, f32[256,16]{1,0:T(8,128)S(1)}, u32[]{:S(2)}) copy-start(f32[256,16]{1,0:T(8,128)S(1)} %copy.187) | copy-start | bytes 49156
  41.0 212.5 %copy-start.16 = (bf16[2048,256]{1,0:T(8,128)(2,1)}, bf16[2048,256]{1,0:T(8,128)(2,1)S(1)}, u32[]{:S(2)}) copy-start(bf16[2048,256]{1,0:T(8,128)(2,1)S(1)} %get-tuple-element.727) | copy-start | bytes 3145732
  259.3 159.9 %all-gather.17.cloned.1.call-start = ((), (), s32[]{:S(2)}) async-start(), calls=%async_computation.15 | async-start | bytes 5242880 | tf_op jit(solution)/shard_map/all_gather | solution.py:151
  260.1 240.0 %all-gather.19.cloned.1.call-start = ((), (), s32[]{:S(2)}) async-start(), calls=%async_computation.16 | async-start | bytes 5242880 | tf_op jit(solution)/shard_map/all_gather | solution.py:150
  260.8 319.5 %all-gather.13.cloned.1.call-start = ((), (), s32[]{:S(2)}) async-start(), calls=%async_computation.11 | async-start | bytes 5242880 | tf_op jit(solution)/shard_map/all_gather | solution.py:150
  261.4 396.0 %reduce-scatter.15.cloned.1.call-start = ((), (), s32[]{:S(2)}) async-start(), calls=%async_computation.17 | async-start | bytes 5242880 | tf_op jit(solution)/shard_map/reduce_scatter | solution.py:176
  261.9 157.3 %copy-start.167 = (f32[128]{0:T(128)S(1)}, f32[128]{0:T(128)}, u32[]{:S(2)}) copy-start(f32[128]{0:T(128)} %param.41) | copy-start | bytes 1540
  522.0 215.0 %reduce-scatter.11.cloned.1.call-start = ((), (), s32[]{:S(2)}) async-start(), calls=%async_computation.12 | async-start | bytes 5242880 | tf_op jit(solution)/shard_map/reduce_scatter | solution.py:176
  602.2 246.6 %all-gather.15.cloned.1.call-start = ((), (), s32[]{:S(2)}) async-start(), calls=%async_computation.13 | async-start | bytes 5242880 | tf_op jit(solution)/shard_map/all_gather | solution.py:184
  766.9 547.4 %copy-start.106 = (f32[2048]{0:T(1024)}, f32[2048]{0:T(1024)S(1)}, u32[]{:S(2)}) copy-start(f32[2048]{0:T(1024)S(1)} %get-tuple-element.749) | copy-start | bytes 24580
  766.9 547.4 %copy-start.108 = (f32[2048]{0:T(1024)}, f32[2048]{0:T(1024)S(1)}, u32[]{:S(2)}) copy-start(f32[2048]{0:T(1024)S(1)} %get-tuple-element.750) | copy-start | bytes 24580
  769.7 159.5 %all-gather.23.cloned.1.call-start = ((), (), s32[]{:S(2)}) async-start(), calls=%async_computation.20 | async-start | bytes 5242880 | tf_op jit(solution)/shard_map/all_gather | solution.py:191
  772.7 251.6 %reduce-scatter.19.cloned.1.call-start = ((), (), s32[]{:S(2)}) async-start(), calls=%async_computation.21 | async-start | bytes 5242880 | tf_op jit(solution)/shard_map/reduce_scatter | solution.py:195
  949.3 161.1 %all-gather.21.cloned.1.call-start = ((), (), s32[]{:S(2)}) async-start(), calls=%async_computation.18 | async-start | bytes 5242880 | tf_op jit(solution)/shard_map/all_gather | solution.py:184
  949.5 358.2 %copy-start.110 = (f32[2048]{0:T(1024)}, f32[2048]{0:T(1024)S(1)}, u32[]{:S(2)}) copy-start(f32[2048]{0:T(1024)S(1)} %get-tuple-element.751) | copy-start | bytes 24580
  949.5 358.2 %copy-start.112 = (f32[2048]{0:T(1024)}, f32[2048]{0:T(1024)S(1)}, u32[]{:S(2)}) copy-start(f32[2048]{0:T(1024)S(1)} %get-tuple-element.752) | copy-start | bytes 24580
  1029.2 161.7 %all-gather.27.cloned.1.call-start = ((), (), s32[]{:S(2)}) async-start(), calls=%async_computation.25 | async-start | bytes 5242880 | tf_op jit(solution)/shard_map/all_gather | solution.py:191
  1029.9 256.3 %reduce-scatter.25.cloned.1.call-start = ((), (), s32[]{:S(2)}) async-start(), calls=%async_computation.26 | async-start | bytes 5242880 | tf_op jit(solution)/shard_map/reduce_scatter | solution.py:195
  1211.2 182.2 %all-gather.29.cloned.1.call-start = ((), (), s32[]{:S(2)}) async-start(), calls=%async_computation.27 | async-start | bytes 5242880 | tf_op jit(solution)/shard_map/all_gather | solution.py:210
  1314.2 159.3 %all-gather.25.cloned.1.call-start = ((), (), s32[]{:S(2)}) async-start(), calls=%async_computation.22 | async-start | bytes 5242880 | tf_op jit(solution)/shard_map/all_gather | solution.py:210
  1320.5 290.7 %all-reduce.15.cloned.1.call-start = ((), (), s32[]{:S(2)}) async-start(), calls=%async_computation.32 | async-start | bytes 2097152 | tf_op jit(solution)/shard_map/psum | solution.py:217
  1484.8 146.0 %reduce-scatter.29.cloned.1.call-start = ((), (), s32[]{:S(2)}) async-start(), calls=%async_computation.29 | async-start | bytes 5242880 | tf_op jit(solution)/shard_map/reduce_scatter | solution.py:262
  1496.7 197.0 %reduce-scatter.23.cloned.1.call-start = ((), (), s32[]{:S(2)}) async-start(), calls=%async_computation.24 | async-start | bytes 5242880 | tf_op jit(solution)/shard_map/reduce_scatter | solution.py:262
  1505.8 585.5 %reduce-scatter.27.cloned.1.call-start = ((), (), s32[]{:S(2)}) async-start(), calls=%async_computation.28 | async-start | bytes 5242880 | tf_op jit(solution)/shard_map/reduce_scatter | solution.py:265
  1517.2 574.2 %reduce-scatter.21.cloned.1.call-start = ((), (), s32[]{:S(2)}) async-start(), calls=%async_computation.23 | async-start | bytes 5242880 | tf_op jit(solution)/shard_map/reduce_scatter | solution.py:265
  1528.5 597.5 %reduce-scatter.17.cloned.1.call-start = ((), (), s32[]{:S(2)}) async-start(), calls=%async_computation.19 | async-start | bytes 5242880 | tf_op jit(solution)/shard_map/reduce_scatter | solution.py:187
  1539.5 594.2 %reduce-scatter.13.cloned.1.call-start = ((), (), s32[]{:S(2)}) async-start(), calls=%async_computation.14 | async-start | bytes 5242880 | tf_op jit(solution)/shard_map/reduce_scatter | solution.py:187
  1549.7 606.1 %all-reduce.11.cloned.1.call-start = ((), (), s32[]{:S(2)}) async-start(), calls=%async_computation.30 | async-start | bytes 140288 | tf_op jit(solution)/shard_map/psum | solution.py:299
  2102.1 286.9 %all-reduce.13.cloned.1.call-start = ((), (), s32[]{:S(2)}) async-start(), calls=%async_computation.31 | async-start | bytes 34603008 | tf_op jit(solution)/shard_map/psum | solution.py:299
  (180 other events, 2347.9 us)
Sparse Core Ops, SparseCore 0:
  259.5 78.7 all-gather.10
  340.4 78.7 all-gather.16
  421.4 78.7 all-gather.18
  501.6 78.7 all-gather.12
  582.5 74.9 reduce-scatter.14
  659.7 77.2 reduce-scatter.10
  769.8 78.9 all-gather.14
  850.4 78.7 all-gather.22
  949.4 74.9 reduce-scatter.18
  1029.3 81.0 all-gather.20
  1112.0 78.7 all-gather.26
  1211.3 74.9 reduce-scatter.24
  1314.3 78.9 all-gather.28
  1394.8 78.7 all-gather.24
  1484.9 50.3 all-reduce.14
  1537.5 76.1 reduce-scatter.28
  1616.4 77.2 reduce-scatter.22
  1696.0 77.2 reduce-scatter.26
  1776.2 77.2 reduce-scatter.20
  1855.7 77.2 reduce-scatter.16
  1935.3 77.2 reduce-scatter.12
  2102.2 53.4 all-reduce.10
  2161.5 227.5 all-reduce.12
where the time goes:
time: 2440 us; the launch traced here: 2430 us
  waiting for transfers between devices  1260 us (52%)
  matrix products  442 us (18%)
  other arithmetic  370 us (15%)
  local copies, waits for them, and re-layouts  253 us (10%)
  blocking collectives  76.4 us (3%)
    psum x2, waiting for transfers between devices, local(): lax.psum((mixer_totals_list[0], mixer_totals_list[1], mixer_totals_list[2...  246 us
    scatter-add x2, other arithmetic, ema_local(): jnp.take(kernel, jnp.maximum(lag, 0), axis=0)  199 us
    all_gather x2, waiting for transfers between devices, local(): ffn_all = lax.all_gather(ffn_low, 'mp', axis=1, tiled=True)  156 us
    all_gather x2, waiting for transfers between devices, local(): lax.all_gather(mixed_low, 'mp', axis=1, tiled=True)  154 us
    reduce_scatter x2, waiting for transfers between devices, local(): lax.psum_scatter(matmul_nt(d_up_pre, up_proj).astype(jnp.bfloat16), 'mp',...  150 us
    all_gather x2, waiting for transfers between devices, local(): grad_all = lax.all_gather(grad_out, 'mp', axis=1, tiled=True)  141 us
    all_gather x2, waiting for transfers between devices, local(): d_act_all = lax.all_gather(d_act_pre, 'mp', axis=1, tiled=True)  136 us
    all_gather x2, waiting for transfers between devices, local(): lax.all_gather(normed_low, 'mp', axis=1, tiled=True)  131 us
  transfers between devices with their start and end apart: 23, of which 17 were waited for; matrix products, arithmetic and copies ran while one was open for 29% of the time, Pallas kernels for 0%

commit v1 on v0

--- a/solution.py
+++ b/solution.py
@@ -8,6 +8,27 @@
 LEN = 2048
 MICRO = 2
 EPS = 1e-05
+
+
+def collect(shard, axis, dim):
+    devices, index, rows = (lax.axis_size(axis), lax.axis_index(axis), shard.shape[dim])
+    ahead = [(i, (i + 1) % devices) for i in range(devices)]
+    left = [(i, (i - 1) % devices) for i in range(devices)]
+    out = jnp.zeros((*shard.shape[:dim], devices * rows, *shard.shape[dim + 1 :]), shard.dtype)
+    out = lax.dynamic_update_slice_in_dim(out, shard, index * rows, axis=dim)
+    from_left = from_right = shard
+    middle = devices // 2
+    for lap in range(1, middle + 1):
+        from_left = lax.ppermute(from_left, axis, ahead)
+        out = lax.dynamic_update_slice_in_dim(
+            out, from_left, (index - lap) % devices * rows, axis=dim
+        )
+        if lap < devices - middle:
+            from_right = lax.ppermute(from_right, axis, left)
+            out = lax.dynamic_update_slice_in_dim(
+                out, from_right, (index + lap) % devices * rows, axis=dim
+            )
+    return out
 
 
 def matmul(left, right):
@@ -148,7 +169,7 @@
         mixed_low = jax.nn.silu(mix_pre).astype(jnp.bfloat16)
         normed_all, mixed_all = (
             lax.all_gather(normed_low, "mp", axis=1, tiled=True),
-            lax.all_gather(mixed_low, "mp", axis=1, tiled=True),
+            collect(mixed_low, "mp", 1),
         )
         shared_pre = matmul(mixed_all, shared_proj)
         shared = jax.nn.silu(shared_pre)

time: 2440 us -> 2340 us (0.959)
  waiting for transfers between devices: 1260 us -> 1100 us
  starting transfers between devices: 3.57 us -> 55.8 us
    all_gather x2 -> x0, waiting for transfers between devices: 154 us -> none  [local(): lax.all_gather(mixed_low, 'mp', axis=1, tiled=True)]
    ppermute x0 -> x6, waiting for transfers between devices: none -> 134 us  [the longest x4 81.9 us: collect(): from_left = lax.ppermute(from_left, axis, ahead)]
    all_gather x2, waiting for transfers between devices: 131 us -> 0.04 us  [local(): lax.all_gather(normed_low, 'mp', axis=1, tiled=True)]
    ppermute x0 -> x6, starting transfers between devices: none -> 52.3 us  [the longest x4 47.5 us: collect(): from_left = lax.ppermute(from_left, axis, ahead)]
    unnamed x401 -> x393, local copies, waits for them, and re-layouts: 75.8 us -> 70.7 us
  transfers between devices with their start and end apart: 23 -> 27, of which waited for: 17 -> 18; matrix products, arithmetic and copies ran while one was open for 29% -> 40% of each run, Pallas kernels for 0% -> 0%
where the time goes in v1:
time: 2340 us; the launch traced here: 2320 us
  waiting for transfers between devices  1100 us (47%)
  matrix products  452 us (19%)
  other arithmetic  360 us (15%)
  local copies, waits for them, and re-layouts  265 us (11%)
  blocking collectives  75.2 us (3%)
  starting transfers between devices  55.8 us (2%)
    psum x2, waiting for transfers between devices, local(): lax.psum((mixer_totals_list[0], mixer_totals_list[1], mixer_totals_list[2...  246 us
    scatter-add x2, other arithmetic, ema_local(): jnp.take(kernel, jnp.maximum(lag, 0), axis=0)  199 us
    all_gather x2, waiting for transfers between devices, local(): ffn_all = lax.all_gather(ffn_low, 'mp', axis=1, tiled=True)  156 us
    reduce_scatter x2, waiting for transfers between devices, local(): lax.psum_scatter(matmul_nt(d_up_pre, up_proj).astype(jnp.bfloat16), 'mp',...  150 us
    all_gather x2, waiting for transfers between devices, local(): grad_all = lax.all_gather(grad_out, 'mp', axis=1, tiled=True)  141 us
    all_gather x2, waiting for transfers between devices, local(): d_act_all = lax.all_gather(d_act_pre, 'mp', axis=1, tiled=True)  136 us
    reduce_scatter x2, waiting for transfers between devices, local(): lax.psum_scatter(matmul(hidden, output_proj).astype(jnp.bfloat16), 'mp',...  117 us
    dot_general x16, matrix products, matmul(): return jnp.dot(left, right, preferred_element_type=jnp.float32)  106 us
  transfers between devices with their start and end apart: 27, of which 18 were waited for; matrix products, arithmetic and copies ran while one was open for 40% of the time, Pallas kernels for 0%

profile of v1, /device:TPU:0, one launch (start us, length us, event | category | flops | bytes accessed | tf_op | source)
XLA Modules:
  0.0 2324.9 jit_solution(11035230540819310518)
XLA Ops:
  10.1 20.8 all-reduce.5
  51.1 21.2 while.64
  82.2 21.2 while.65
  116.3 67.0 %gather_fusion = f32[16384,256]{1,0:T(8,128)} fusion(f32[128,256]{1,0:T(8,128)S(1)} %copy.189, s32[16384]{0:T(1024)} %broadcast_clamp_fusion), kind=kCustom, calls=%fused_computation.clone | custom fusion | bytes 33619968 | tf_op jit(solution)/shard_map/jvp(jit(_take))/gather | solution.py:81
  183.2 18.0 copy.190
  267.7 24.5 %collective-permute-done.3 = bf16[2048,256]{1,0:T(8,128)(2,1)} collective-permute-done((bf16[2048,256]{1,0:T(8,128)(2,1)S(1)}, bf16[2048,256]{1,0:T(8,128)(2,1)}, u32[]{:S(2)}, u32[]{:S(2)}) %collective-permute-start.3) | collective-permute-done | bytes 1048608 | tf_op jit(solution)/shard_map/ppermute | solution.py:22
  298.5 38.5 %collective-permute-done = bf16[2048,256]{1,0:T(8,128)(2,1)} collective-permute-done((bf16[2048,256]{1,0:T(8,128)(2,1)}, bf16[2048,256]{1,0:T(8,128)(2,1)}, u32[]{:S(2)}, u32[]{:S(2)}) %collective-permute-start) | collective-permute-done | bytes 1048608 | tf_op jit(solution)/shard_map/ppermute | solution.py:22
  337.0 40.7 %collective-permute-start.2 = (bf16[2048,256]{1,0:T(8,128)(2,1)}, bf16[2048,256]{1,0:T(8,128)(2,1)S(1)}, u32[]{:S(2)}, u32[]{:S(2)}) collective-permute-start(bf16[2048,256]{1,0:T(8,128)(2,1)} %collective-permute-done), channel_id=1, source_target_pairs={{0,1},{1,2},{2,3},{3,0},{4,5},{5,6},{6,7},{7,4},{8,9},{9,10},{10,1... | collective-permute-start | bytes 3145736 | tf_op jit(solution)/shard_map/ppermute | solution.py:22
  384.6 51.9 %collective-permute-done.1 = bf16[2048,256]{1,0:T(8,128)(2,1)} collective-permute-done((bf16[2048,256]{1,0:T(8,128)(2,1)}, bf16[2048,256]{1,0:T(8,128)(2,1)}, u32[]{:S(2)}, u32[]{:S(2)}) %collective-permute-start.1) | collective-permute-done | bytes 1048608 | tf_op jit(solution)/shard_map/ppermute | solution.py:27
  523.5 42.3 %reduce-scatter.15.cloned.1.call-done = bf16[2048,256]{1,0:T(8,128)(2,1)} async-done(((bf16[2048,1024]{1,0:T(8,128)(2,1)}), bf16[2048,256]{1,0:T(8,128)(2,1)}) %reduce-scatter.15.cloned.1.call-update) | async-done | bytes 1048592 | tf_op jit(solution)/shard_map/reduce_scatter | solution.py:197
  570.9 74.5 %reduce-scatter.11.cloned.1.call-done = bf16[2048,256]{1,0:T(8,128)(2,1)} async-done(((bf16[2048,1024]{1,0:T(8,128)(2,1)}), bf16[2048,256]{1,0:T(8,128)(2,1)}) %reduce-scatter.11.cloned.1.call-update) | async-done | bytes 1048592 | tf_op jit(solution)/shard_map/reduce_scatter | solution.py:197
  658.1 18.2 all-reduce.4
  682.7 75.6 %all-gather.11.cloned.1.call-done = bf16[2048,1024]{1,0:T(8,128)(2,1)} async-done(((bf16[2048,256]{1,0:T(8,128)(2,1)}), bf16[2048,1024]{1,0:T(8,128)(2,1)}) %all-gather.11.cloned.1.call-update) | async-done | bytes 4194320 | tf_op jit(solution)/shard_map/all_gather | solution.py:205
  769.0 69.4 %all-gather.17.cloned.1.call-done = bf16[2048,1024]{1,0:T(8,128)(2,1)} async-done(((bf16[2048,256]{1,0:T(8,128)(2,1)}), bf16[2048,1024]{1,0:T(8,128)(2,1)}) %all-gather.17.cloned.1.call-update) | async-done | bytes 4194320 | tf_op jit(solution)/shard_map/all_gather | solution.py:212
  858.8 74.8 %reduce-scatter.19.cloned.1.call-done = bf16[2048,256]{1,0:T(8,128)(2,1)} async-done(((bf16[2048,1024]{1,0:T(8,128)(2,1)}), bf16[2048,256]{1,0:T(8,128)(2,1)}) %reduce-scatter.19.cloned.1.call-update) | async-done | bytes 1048592 | tf_op jit(solution)/shard_map/reduce_scatter | solution.py:216
  939.3 80.4 %all-gather.15.cloned.1.call-done = bf16[2048,1024]{1,0:T(8,128)(2,1)} async-done(((bf16[2048,256]{1,0:T(8,128)(2,1)}), bf16[2048,1024]{1,0:T(8,128)(2,1)}) %all-gather.15.cloned.1.call-update) | async-done | bytes 4194320 | tf_op jit(solution)/shard_map/all_gather | solution.py:205
  1028.8 71.4 %all-gather.21.cloned.1.call-done = bf16[2048,1024]{1,0:T(8,128)(2,1)} async-done(((bf16[2048,256]{1,0:T(8,128)(2,1)}), bf16[2048,1024]{1,0:T(8,128)(2,1)}) %all-gather.21.cloned.1.call-update) | async-done | bytes 4194320 | tf_op jit(solution)/shard_map/all_gather | solution.py:212
  1120.6 74.8 %reduce-scatter.25.cloned.1.call-done = bf16[2048,256]{1,0:T(8,128)(2,1)} async-done(((bf16[2048,1024]{1,0:T(8,128)(2,1)}), bf16[2048,256]{1,0:T(8,128)(2,1)}) %reduce-scatter.25.cloned.1.call-update) | async-done | bytes 1048592 | tf_op jit(solution)/shard_map/reduce_scatter | solution.py:216
  1198.7 18.2 all-reduce.3
  1235.9 66.7 %all-gather.23.cloned.1.call-done = bf16[2048,1024]{1,0:T(8,128)(2,1)} async-done(((bf16[2048,256]{1,0:T(8,128)(2,1)}), bf16[2048,1024]{1,0:T(8,128)(2,1)}) %all-gather.23.cloned.1.call-update) | async-done | bytes 4194320 | tf_op jit(solution)/shard_map/all_gather | solution.py:231
  1313.6 69.1 %all-gather.19.cloned.1.call-done = bf16[2048,1024]{1,0:T(8,128)(2,1)} async-done(((bf16[2048,256]{1,0:T(8,128)(2,1)}), bf16[2048,1024]{1,0:T(8,128)(2,1)}) %all-gather.19.cloned.1.call-update) | async-done | bytes 4194320 | tf_op jit(solution)/shard_map/all_gather | solution.py:231
  1559.2 23.4 %while.66 = (s32[]{:T(128)}, f32[256,16]{0,1:T(8,128)S(1)}, f32[1,256,16]{1,2,0:T(8,128)S(1)}, f32[16,1,256,16]{2,3,1,0:T(8,128)S(1)}, f32[16,1,256,16]{2,3,1,0:...) while((s32[]{:T(128)}, f32[256,16]{0,1:T(8,128)S(1)}, ...), condition=%wide.region_39.41_spmd.clone, body=%wide.region_38.40_spmd.clone.sunk | while | flops 32772 | bytes 165516 | solution.py:90
  1582.6 19.6 reduce-scatter.29.cloned.1.call-done
  1633.2 17.5 fusion.1
  1662.1 17.7 fusion
  1704.8 17.9 copy.254
  1722.7 99.6 %scatter_custom_fusion = f32[128,256]{1,0:T(8,128)} fusion(s32[16384]{0:T(1024)S(1)} %fusion.236, f32[16384,256]{1,0:T(8,128)} %bitcast.422, f32[]{:T(128)} %constant.194.clone.1), kind=kCustom, calls=%fused_computation.354 | custom fusion | flops 4194304 | bytes 131584 | tf_op jit(solution)/shard_map/transpose(jvp(jit(_take)))/scatter-add | solution.py:81
  1824.0 16.8 select_bitcast_fusion
  1840.8 17.9 copy.255
  1858.7 99.4 %scatter_custom_fusion.1 = f32[128,256]{1,0:T(8,128)} fusion(s32[16384]{0:T(1024)S(1)} %fusion.236, f32[16384,256]{1,0:T(8,128)} %bitcast.421, f32[]{:T(128)} %constant.194.clone.1), kind=kCustom, calls=%fused_computation.352 | custom fusion | flops 4194304 | bytes 131584 | tf_op jit(solution)/shard_map/transpose(jvp(jit(_take)))/scatter-add | solution.py:81
  2006.3 18.0 all-reduce.2
  2054.5 233.3 %all-reduce.13.cloned.1.call-done = (f32[1024,128]{1,0:T(8,128)}, f32[1024,512]{1,0:T(8,128)}, f32[1024,512]{1,0:T(8,128)}, f32[1024,256]{1,0:T(8,128)}, f32[102...) async-done(((f32[1024,128]{1,0:T(8,128)}, f32[1024,512]{1,0:T(8,128)}, f32[1024,512]{1,0:T(8,128)}, f32[1024,256]{1,0:T(8,128)}, ...) | async-done | bytes 17301520 | tf_op jit(solution)/shard_map/psum | solution.py:320
  (797 shorter events, 765.6 us)
Async XLA Ops:
  7.2 751.1 %copy-start = (bf16[1024,1024]{1,0:T(8,128)(2,1)S(1)}, bf16[1024,1024]{1,0:T(8,128)(2,1)}, u32[]{:S(2)}) copy-start(bf16[1024,1024]{1,0:T(8,128)(2,1)} %param.48) | copy-start | bytes 6291460
  7.2 461.6 %all-gather.13.cloned.1.call-start = ((), (), s32[]{:S(2)}) async-start(), calls=%async_computation.14 | async-start | bytes 5242880 | tf_op jit(solution)/shard_map/all_gather | solution.py:171
  35.2 457.7 %all-gather.9.cloned.1.call-start = ((), (), s32[]{:S(2)}) async-start(), calls=%async_computation.10 | async-start | bytes 5242880 | tf_op jit(solution)/shard_map/all_gather | solution.py:171
  257.2 35.0 %collective-permute-start.3 = (bf16[2048,256]{1,0:T(8,128)(2,1)S(1)}, bf16[2048,256]{1,0:T(8,128)(2,1)}, u32[]{:S(2)}, u32[]{:S(2)}) collective-permute-start(bf16[2048,256]{1,0:T(8,128)(2,1)S(1)} %get-tuple-element.712), channel_id=1, source_target_pairs={{0,1},{1,2},{2,3},{3,0},{4,5},{5,6},{6,7},{7,4},{8,9},{9,10},{10,1... | collective-permute-start | bytes 3145736 | tf_op jit(solution)/shard_map/ppermute | solution.py:22
  262.3 74.7 %collective-permute-start = (bf16[2048,256]{1,0:T(8,128)(2,1)}, bf16[2048,256]{1,0:T(8,128)(2,1)}, u32[]{:S(2)}, u32[]{:S(2)}) collective-permute-start(bf16[2048,256]{1,0:T(8,128)(2,1)} %get-tuple-element.709), channel_id=1, source_target_pairs={{0,1},{1,2},{2,3},{3,0},{4,5},{5,6},{6,7},{7,4},{8,9},{9,10},{10,1... | collective-permute-start | bytes 3145736 | tf_op jit(solution)/shard_map/ppermute | solution.py:22
  262.8 119.4 %collective-permute-start.4 = (bf16[2048,256]{1,0:T(8,128)(2,1)S(1)}, bf16[2048,256]{1,0:T(8,128)(2,1)}, u32[]{:S(2)}, u32[]{:S(2)}) collective-permute-start(bf16[2048,256]{1,0:T(8,128)(2,1)S(1)} %get-tuple-element.712), channel_id=1, source_target_pairs={{0,3},{1,0},{2,1},{3,2},{4,7},{5,4},{6,5},{7,6},{8,11},{9,8},{10,9... | collective-permute-start | bytes 3145736 | tf_op jit(solution)/shard_map/ppermute | solution.py:27
  266.2 299.6 %reduce-scatter.15.cloned.1.call-start = ((), (), s32[]{:S(2)}) async-start(), calls=%async_computation.15 | async-start | bytes 5242880 | tf_op jit(solution)/shard_map/reduce_scatter | solution.py:197
  266.2 170.2 %collective-permute-start.1 = (bf16[2048,256]{1,0:T(8,128)(2,1)}, bf16[2048,256]{1,0:T(8,128)(2,1)}, u32[]{:S(2)}, u32[]{:S(2)}) collective-permute-start(bf16[2048,256]{1,0:T(8,128)(2,1)} %get-tuple-element.709), channel_id=1, source_target_pairs={{0,3},{1,0},{2,1},{3,2},{4,7},{5,4},{6,5},{7,6},{8,11},{9,8},{10,9... | collective-permute-start | bytes 3145736 | tf_op jit(solution)/shard_map/ppermute | solution.py:27
  292.1 150.5 %collective-permute-start.5 = (bf16[2048,256]{1,0:T(8,128)(2,1)}, bf16[2048,256]{1,0:T(8,128)(2,1)}, u32[]{:S(2)}, u32[]{:S(2)}) collective-permute-start(bf16[2048,256]{1,0:T(8,128)(2,1)} %collective-permute-done.3), channel_id=1, source_target_pairs={{0,1},{1,2},{2,3},{3,0},{4,5},{5,6},{6,7},{7,4},{8,9},{9,10},{10,1... | collective-permute-start | bytes 3145736 | tf_op jit(solution)/shard_map/ppermute | solution.py:22
  337.0 122.8 %collective-permute-start.2 = (bf16[2048,256]{1,0:T(8,128)(2,1)}, bf16[2048,256]{1,0:T(8,128)(2,1)S(1)}, u32[]{:S(2)}, u32[]{:S(2)}) collective-permute-start(bf16[2048,256]{1,0:T(8,128)(2,1)} %collective-permute-done), channel_id=1, source_target_pairs={{0,1},{1,2},{2,3},{3,0},{4,5},{5,6},{6,7},{7,4},{8,9},{9,10},{10,1... | collective-permute-start | bytes 3145736 | tf_op jit(solution)/shard_map/ppermute | solution.py:22
  490.7 154.7 %reduce-scatter.11.cloned.1.call-start = ((), (), s32[]{:S(2)}) async-start(), calls=%async_computation.11 | async-start | bytes 5242880 | tf_op jit(solution)/shard_map/reduce_scatter | solution.py:197
  517.8 240.5 %all-gather.11.cloned.1.call-start = ((), (), s32[]{:S(2)}) async-start(), calls=%async_computation.12 | async-start | bytes 5242880 | tf_op jit(solution)/shard_map/all_gather | solution.py:205
  676.3 547.2 %copy-start.101 = (f32[2048]{0:T(1024)}, f32[2048]{0:T(1024)S(1)}, u32[]{:S(2)}) copy-start(f32[2048]{0:T(1024)S(1)} %get-tuple-element.749) | copy-start | bytes 24580
  676.4 547.2 %copy-start.103 = (f32[2048]{0:T(1024)}, f32[2048]{0:T(1024)S(1)}, u32[]{:S(2)}) copy-start(f32[2048]{0:T(1024)S(1)} %get-tuple-element.750) | copy-start | bytes 24580
  679.2 159.3 %all-gather.17.cloned.1.call-start = ((), (), s32[]{:S(2)}) async-start(), calls=%async_computation.18 | async-start | bytes 5242880 | tf_op jit(solution)/shard_map/all_gather | solution.py:212
  682.2 251.4 %reduce-scatter.19.cloned.1.call-start = ((), (), s32[]{:S(2)}) async-start(), calls=%async_computation.19 | async-start | bytes 5242880 | tf_op jit(solution)/shard_map/reduce_scatter | solution.py:216
  858.6 161.2 %all-gather.15.cloned.1.call-start = ((), (), s32[]{:S(2)}) async-start(), calls=%async_computation.16 | async-start | bytes 5242880 | tf_op jit(solution)/shard_map/all_gather | solution.py:205
  858.8 358.1 %copy-start.105 = (f32[2048]{0:T(1024)}, f32[2048]{0:T(1024)S(1)}, u32[]{:S(2)}) copy-start(f32[2048]{0:T(1024)S(1)} %get-tuple-element.751) | copy-start | bytes 24580
  858.8 358.1 %copy-start.107 = (f32[2048]{0:T(1024)}, f32[2048]{0:T(1024)S(1)}, u32[]{:S(2)}) copy-start(f32[2048]{0:T(1024)S(1)} %get-tuple-element.752) | copy-start | bytes 24580
  938.5 161.7 %all-gather.21.cloned.1.call-start = ((), (), s32[]{:S(2)}) async-start(), calls=%async_computation.23 | async-start | bytes 5242880 | tf_op jit(solution)/shard_map/all_gather | solution.py:212
  939.2 256.2 %reduce-scatter.25.cloned.1.call-start = ((), (), s32[]{:S(2)}) async-start(), calls=%async_computation.24 | async-start | bytes 5242880 | tf_op jit(solution)/shard_map/reduce_scatter | solution.py:216
  1120.4 182.2 %all-gather.23.cloned.1.call-start = ((), (), s32[]{:S(2)}) async-start(), calls=%async_computation.25 | async-start | bytes 5242880 | tf_op jit(solution)/shard_map/all_gather | solution.py:231
  1223.4 159.3 %all-gather.19.cloned.1.call-start = ((), (), s32[]{:S(2)}) async-start(), calls=%async_computation.20 | async-start | bytes 5242880 | tf_op jit(solution)/shard_map/all_gather | solution.py:231
  1229.7 294.8 %all-reduce.15.cloned.1.call-start = ((), (), s32[]{:S(2)}) async-start(), calls=%async_computation.30 | async-start | bytes 2097152 | tf_op jit(solution)/shard_map/psum | solution.py:238
  1393.9 150.6 %reduce-scatter.23.cloned.1.call-start = ((), (), s32[]{:S(2)}) async-start(), calls=%async_computation.22 | async-start | bytes 5242880 | tf_op jit(solution)/shard_map/reduce_scatter | solution.py:283
  1405.6 196.7 %reduce-scatter.29.cloned.1.call-start = ((), (), s32[]{:S(2)}) async-start(), calls=%async_computation.27 | async-start | bytes 5242880 | tf_op jit(solution)/shard_map/reduce_scatter | solution.py:283
  1414.7 575.5 %reduce-scatter.27.cloned.1.call-start = ((), (), s32[]{:S(2)}) async-start(), calls=%async_computation.26 | async-start | bytes 5242880 | tf_op jit(solution)/shard_map/reduce_scatter | solution.py:286
  1426.1 564.2 %reduce-scatter.21.cloned.1.call-start = ((), (), s32[]{:S(2)}) async-start(), calls=%async_computation.21 | async-start | bytes 5242880 | tf_op jit(solution)/shard_map/reduce_scatter | solution.py:286
  1437.4 586.9 %reduce-scatter.17.cloned.1.call-start = ((), (), s32[]{:S(2)}) async-start(), calls=%async_computation.17 | async-start | bytes 5242880 | tf_op jit(solution)/shard_map/reduce_scatter | solution.py:208
  1448.3 583.7 %reduce-scatter.13.cloned.1.call-start = ((), (), s32[]{:S(2)}) async-start(), calls=%async_computation.13 | async-start | bytes 5242880 | tf_op jit(solution)/shard_map/reduce_scatter | solution.py:208
  1458.4 596.2 %all-reduce.11.cloned.1.call-start = ((), (), s32[]{:S(2)}) async-start(), calls=%async_computation.28 | async-start | bytes 140288 | tf_op jit(solution)/shard_map/psum | solution.py:320
  2001.0 286.8 %all-reduce.13.cloned.1.call-start = ((), (), s32[]{:S(2)}) async-start(), calls=%async_computation.29 | async-start | bytes 34603008 | tf_op jit(solution)/shard_map/psum | solution.py:320
  (180 other events, 2044.8 us)
Sparse Core Ops, SparseCore 0:
  35.3 78.7 all-gather.12
  266.3 155.6 all-gather.8
  490.8 74.9 reduce-scatter.14
  568.1 77.2 reduce-scatter.10
  679.3 78.9 all-gather.10
  759.7 78.7 all-gather.16
  858.7 74.9 reduce-scatter.18
  938.6 81.0 all-gather.14
  1021.4 78.7 all-gather.20
  1120.5 74.9 reduce-scatter.24
  1223.6 78.9 all-gather.22
  1304.0 78.7 all-gather.18
  1394.0 50.3 all-reduce.14
  1446.7 76.1 reduce-scatter.22
  1525.0 77.2 reduce-scatter.28
  1604.5 77.2 reduce-scatter.26
  1684.5 77.2 reduce-scatter.20
  1764.1 77.2 reduce-scatter.16
  1843.7 77.2 reduce-scatter.12
  2001.1 53.3 all-reduce.10
  2060.2 227.5 all-reduce.12
